TPU v7x, 32 devices: a whole 2x2x4 slice. The times are simulated.
32 devices in a mesh: gx: 8 (over z, y), gy: 4 (over x, core).
Axes of the slice: x: 2, y: 2, z: 4, core: 2. Of those that a mesh axis runs over, the one named last changes fastest.
Arguments:
- tokens: bfloat16 [48, 24, 8, 384], P('gx', 'gy'), may hold values from -6 to 6
- upstream: bfloat16 [48, 24, 8, 384], P('gx', 'gy'), may hold values from -41 to 41
- window_labels: int32 [48, 24, 8], P('gx', 'gy'), may hold values from 0 to 2
- ln1_gain: float32 [384], replicated, may hold values from 0.5 to 1.5
- w_qkv: bfloat16 [384, 1152], replicated, as said below
- w_proj: bfloat16 [384, 384], replicated, may hold values from -0.3125 to 0.3125
- ln2_gain: float32 [384], replicated, may hold values from 0.5 to 1.5
- w_fc1: bfloat16 [384, 1536], replicated, may hold values from -0.3125 to 0.3125
- b_fc1: float32 [1536], replicated, may hold values from -3 to 3
- w_fc2: bfloat16 [1536, 384], replicated, may hold values from -0.15625 to 0.15625
Outputs:
- d_tokens: bfloat16 [48, 24, 8, 384], P('gx', 'gy')
- g_ln1: float32 [384], replicated
- g_qkv: bfloat16 [384, 1152], replicated
- g_proj: bfloat16 [384, 384], replicated
- g_ln2: float32 [384], replicated
- g_fc1: bfloat16 [384, 1536], replicated
- g_bfc1: float32 [1536], replicated
- g_fc2: bfloat16 [1536, 384], replicated
Inputs may be any that keep to these rules, and one draw needn't show every extreme that they name: `w_qkv`: entries at most 28 / sqrt(384) in magnitude.
All inputs are finite; a program needn't handle non-finite values.
Results may differ from a plain program's by a relative error of at most 0.019.
Values may be sent and summed in bfloat16 or wider, within the bound.
No kernel may reach another device: no remote copies, remote signals or barrier semaphores. Data moves between devices by JAX's collectives and lax.ppermute only.
A program may use at most 128 MiB of HBM per device.

v0:
```python
import math
import jax
import jax.numpy as jnp
from jax import lax
from jax.sharding import PartitionSpec as P

HD = 32
WZ = 8
EPS = 1e-05
CUBIC = 0.044715
ROOT_TWO_PI = math.sqrt(2.0 / math.pi)


def shifted(shard, axis, by):
    size = lax.axis_size(axis)
    return lax.ppermute(shard, axis, [(i, (i + by) % size) for i in range(size)])


def row_stats(values):
    row_mean = jnp.mean(values, axis=-1, keepdims=True)
    center = values - row_mean
    variance = jnp.mean(center * center, axis=-1, keepdims=True)
    inv_std = lax.rsqrt(variance + EPS)
    return (center * inv_std, inv_std)


def norm_back(incoming, normed, inv_std, gain_vec):
    scaled = incoming * gain_vec
    first_mean = jnp.mean(scaled, axis=-1, keepdims=True)
    second_mean = jnp.mean(scaled * normed, axis=-1, keepdims=True)
    flat_terms = (incoming * normed).reshape(-1, incoming.shape[-1])
    return (inv_std * (scaled - first_mean - normed * second_mean), jnp.sum(flat_terms, axis=0))


def gelu_pair(preact):
    cubic_arg = ROOT_TWO_PI * (preact + CUBIC * preact * preact * preact)
    tanh_value = jnp.tanh(cubic_arg)
    gelu_value = 0.5 * preact * (1.0 + tanh_value)
    gelu_slope = 0.5 * (1.0 + tanh_value) + 0.5 * preact * (
        1.0 - tanh_value * tanh_value
    ) * ROOT_TWO_PI * (1.0 + 3.0 * CUBIC * preact * preact)
    return (gelu_value, gelu_slope)


def to_windows(grid_tile, win_depth):
    tile_x, tile_y, tile_z = grid_tile.shape[:3]
    trailing = grid_tile.shape[3:]
    blocks = tile_z // win_depth
    shaped = grid_tile.reshape((tile_x, tile_y, blocks, win_depth) + trailing)
    axes_order = (2, 0, 1, 3) + tuple(range(4, 4 + len(trailing)))
    return shaped.transpose(axes_order).reshape((blocks, tile_x * tile_y * win_depth) + trailing)


def from_windows(win_rows, tile_x, tile_y, win_depth):
    blocks = win_rows.shape[0]
    trailing = win_rows.shape[2:]
    shaped = win_rows.reshape((blocks, tile_x, tile_y, win_depth) + trailing)
    axes_order = (1, 2, 0, 3) + tuple(range(4, 4 + len(trailing)))
    return shaped.transpose(axes_order).reshape((tile_x, tile_y, blocks * win_depth) + trailing)


def roll_ahead(grid_tile, dim_x):
    half_size = grid_tile.shape[dim_x] // 2
    arrived = shifted(lax.slice_in_dim(grid_tile, 0, half_size, axis=dim_x), "gx", -1)
    grid_tile = jnp.concatenate(
        (lax.slice_in_dim(grid_tile, half_size, grid_tile.shape[dim_x], axis=dim_x), arrived),
        axis=dim_x,
    )
    dim_y = dim_x + 1
    half_size = grid_tile.shape[dim_y] // 2
    arrived = shifted(lax.slice_in_dim(grid_tile, 0, half_size, axis=dim_y), "gy", -1)
    grid_tile = jnp.concatenate(
        (lax.slice_in_dim(grid_tile, half_size, grid_tile.shape[dim_y], axis=dim_y), arrived),
        axis=dim_y,
    )
    return jnp.roll(grid_tile, -(WZ // 2), axis=dim_x + 2)


def unroll_wide(grid_tile):
    grid_tile = jnp.roll(grid_tile, WZ // 2, axis=2)
    size_x = grid_tile.shape[0]
    keep_x = size_x - size_x // 2
    arrived = shifted(grid_tile[keep_x:].astype(jnp.bfloat16), "gx", 1).astype(jnp.float32)
    grid_tile = jnp.concatenate((arrived, grid_tile[:keep_x]), axis=0)
    size_y = grid_tile.shape[1]
    keep_y = size_y - size_y // 2
    arrived = shifted(grid_tile[:, keep_y:].astype(jnp.bfloat16), "gy", 1).astype(jnp.float32)
    return jnp.concatenate((arrived, grid_tile[:, :keep_y]), axis=1)


def attend_forward(h_rows, region_codes, w_qkv, w_proj):
    blocks, length, model_width = h_rows.shape
    head_count = model_width // HD
    score_scale = HD ** (-0.5)
    packed = jnp.dot(
        h_rows.reshape(-1, model_width), w_qkv, preferred_element_type=jnp.float32
    ).astype(jnp.bfloat16)
    packed = packed.reshape(blocks, length, 3, head_count, HD)
    queries = packed[:, :, 0]
    key_part = packed[:, :, 1]
    val_part = packed[:, :, 2]
    allowed = (region_codes[:, :, None] == region_codes[:, None, :])[:, None]
    scores = (
        jnp.einsum("bqhe,bkhe->bhqk", queries, key_part, preferred_element_type=jnp.float32)
        * score_scale
    )
    scores = jnp.where(allowed, scores, -1e30)
    highest = jnp.max(scores, axis=-1, keepdims=True)
    exp_scores = jnp.exp(scores - highest)
    probs = exp_scores / jnp.sum(exp_scores, axis=-1, keepdims=True)
    probs_low = probs.astype(jnp.bfloat16)
    head_mix = jnp.einsum(
        "bhqk,bkhe->bqhe", probs_low, val_part, preferred_element_type=jnp.float32
    ).astype(jnp.bfloat16)
    head_mix = head_mix.reshape(blocks * length, model_width)
    attn_out = jnp.dot(head_mix, w_proj, preferred_element_type=jnp.float32).reshape(
        blocks, length, model_width
    )
    return (attn_out, (queries, key_part, val_part, probs, probs_low, head_mix))


def attend_backward(grad_rows, saved, h_rows, w_qkv, w_proj):
    queries, key_part, val_part, probs, probs_low, head_mix = saved
    blocks, length, model_width = grad_rows.shape
    head_count = model_width // HD
    score_scale = HD ** (-0.5)
    flat_grad = grad_rows.reshape(-1, model_width)
    grad_proj = jnp.dot(head_mix.T, flat_grad, preferred_element_type=jnp.float32)
    grad_mix = jnp.dot(flat_grad, w_proj.T, preferred_element_type=jnp.float32).astype(jnp.bfloat16)
    grad_mix = grad_mix.reshape(blocks, length, head_count, HD)
    grad_probs = jnp.einsum(
        "bqhe,bkhe->bhqk", grad_mix, val_part, preferred_element_type=jnp.float32
    )
    grad_val = jnp.einsum(
        "bhqk,bqhe->bkhe", probs_low, grad_mix, preferred_element_type=jnp.float32
    )
    grad_scores = probs * (grad_probs - jnp.sum(probs * grad_probs, axis=-1, keepdims=True))
    grad_low = (grad_scores * score_scale).astype(jnp.bfloat16)
    grad_query = jnp.einsum(
        "bhqk,bkhe->bqhe", grad_low, key_part, preferred_element_type=jnp.float32
    )
    grad_key = jnp.einsum("bhqk,bqhe->bkhe", grad_low, queries, preferred_element_type=jnp.float32)
    grad_packed = (
        jnp.stack((grad_query, grad_key, grad_val), axis=2)
        .astype(jnp.bfloat16)
        .reshape(-1, 3 * model_width)
    )
    grad_qkv = jnp.dot(
        h_rows.reshape(-1, model_width).T, grad_packed, preferred_element_type=jnp.float32
    )
    grad_input = jnp.dot(grad_packed, w_qkv.T, preferred_element_type=jnp.float32).reshape(
        blocks, length, model_width
    )
    return (grad_input, grad_qkv, grad_proj)


def mlp_backward(wide_tok, attn_out, up_tok, ln2_gain, w_fc1, b_fc1, w_fc2):
    model_width = wide_tok.shape[-1]
    lead_shape = wide_tok.shape[:-1]
    resid_mid = (wide_tok + attn_out).astype(jnp.bfloat16)
    normed, inv_std = row_stats(resid_mid.astype(jnp.float32))
    hidden_in = (normed * ln2_gain).astype(jnp.bfloat16).reshape(-1, model_width)
    preact = jnp.dot(hidden_in, w_fc1, preferred_element_type=jnp.float32) + b_fc1
    gelu_value, gelu_slope = gelu_pair(preact)
    hidden = gelu_value.astype(jnp.bfloat16)
    flat_up = up_tok.reshape(-1, model_width)
    grad_fc2 = jnp.dot(hidden.T, flat_up, preferred_element_type=jnp.float32)
    grad_pre = (jnp.dot(flat_up, w_fc2.T, preferred_element_type=jnp.float32) * gelu_slope).astype(
        jnp.bfloat16
    )
    grad_bias = jnp.sum(grad_pre.astype(jnp.float32), axis=0)
    grad_fc1 = jnp.dot(hidden_in.T, grad_pre, preferred_element_type=jnp.float32)
    grad_norm = jnp.dot(grad_pre, w_fc1.T, preferred_element_type=jnp.float32).reshape(
        lead_shape + (model_width,)
    )
    grad_mid, grad_gain2 = norm_back(grad_norm, normed, inv_std, ln2_gain)
    grad_res = up_tok.astype(jnp.float32) + grad_mid
    return (grad_res, (grad_gain2, grad_fc1, grad_bias, grad_fc2))


def body(tokens, upstream, window_labels, ln1_gain, w_qkv, w_proj, ln2_gain, w_fc1, b_fc1, w_fc2):
    tile_x, tile_y, tile_z, model_width = tokens.shape
    last_x = lax.axis_index("gx") == lax.axis_size("gx") - 1
    last_y = lax.axis_index("gy") == lax.axis_size("gy") - 1
    wrap_x = (last_x & (jnp.arange(tile_x) >= tile_x - tile_x // 2)).astype(jnp.int32)
    wrap_y = (last_y & (jnp.arange(tile_y) >= tile_y - tile_y // 2)).astype(jnp.int32)
    wrap_z = (jnp.arange(tile_z) >= tile_z - WZ // 2).astype(jnp.int32)
    code_tile = (
        window_labels * 8
        + wrap_x[:, None, None] * 4
        + wrap_y[None, :, None] * 2
        + wrap_z[None, None, :]
    )
    region_codes = to_windows(code_tile, WZ)
    wide_tok = tokens.astype(jnp.float32)
    normed_first, inv_first = row_stats(wide_tok)
    h_first = (normed_first * ln1_gain).astype(jnp.bfloat16)
    h_rows = to_windows(roll_ahead(h_first, 0), WZ)
    attn_rows, saved = attend_forward(h_rows, region_codes, w_qkv, w_proj)
    attn_tile = unroll_wide(from_windows(attn_rows, tile_x, tile_y, WZ))
    grad_res, mlp_grads = mlp_backward(wide_tok, attn_tile, upstream, ln2_gain, w_fc1, b_fc1, w_fc2)
    grad_attn = grad_res.astype(jnp.bfloat16)
    grad_rows = to_windows(roll_ahead(grad_attn, 0), WZ)
    input_rows, grad_qkv, grad_proj = attend_backward(grad_rows, saved, h_rows, w_qkv, w_proj)
    grad_first = unroll_wide(from_windows(input_rows, tile_x, tile_y, WZ))
    grad_tok, grad_gain1 = norm_back(grad_first, normed_first, inv_first, ln1_gain)
    result = (grad_res + grad_tok).astype(jnp.bfloat16)
    grad_gain2, grad_fc1, grad_bias, grad_fc2 = mlp_grads
    local_grads = (grad_gain1, grad_qkv, grad_proj, grad_gain2, grad_fc1, grad_bias, grad_fc2)
    param_total = 0
    for grad_term in local_grads:
        param_total = param_total + math.prod(grad_term.shape)
    summed = lax.psum(
        (
            local_grads[0],
            local_grads[1],
            local_grads[2],
            local_grads[3],
            local_grads[4],
            local_grads[5],
            local_grads[6],
        ),
        ("gx", "gy"),
    )
    square_sum = jnp.zeros((), jnp.float32)
    for grad_term in summed:
        square_sum = square_sum + jnp.sum(grad_term * grad_term)
    factor = math.sqrt(param_total) * lax.rsqrt(square_sum)
    scaled = tuple((grad_term * factor for grad_term in summed))
    return (
        result,
        scaled[0],
        scaled[1].astype(jnp.bfloat16),
        scaled[2].astype(jnp.bfloat16),
        scaled[3],
        scaled[4].astype(jnp.bfloat16),
        scaled[5],
        scaled[6].astype(jnp.bfloat16),
    )


def solution(mesh):
    return jax.shard_map(
        body,
        mesh=mesh,
        in_specs=(
            P("gx", "gy", None, None),
            P("gx", "gy", None, None),
            P("gx", "gy", None),
            P(),
            P(),
            P(),
            P(),
            P(),
            P(),
            P(),
        ),
        out_specs=(P("gx", "gy", None, None), P(), P(), P(), P(), P(), P(), P()),
        check_vma=False,
    )
```

profile of v0, /device:TPU:0, one launch (start us, length us, event | category | flops | bytes accessed | tf_op | source)
XLA Modules:
  0.0 288.3 jit_solution(15074106265206905131)
XLA Ops:
  10.7 6.1 %collective-permute-start = (bf16[3,6,8,384]{3,2,1,0:T(8,128)(2,1)S(1)}, bf16[3,6,8,384]{3,2,1,0:T(8,128)(2,1)S(1)}, u32[]{:S(2)}, u32[]{:S(2)}) collective-permute-start(bf16[3,6,8,384]{3,2,1,0:T(8,128)(2,1)S(1)} %get-tuple-element.33), channel_id=1, source_target_pairs={{0,28},{4,0},{8,4},{12,8},{16,12},{20,16},{24,20},{28,24},{1,29},{... | collective-permute-start | bytes 331784 | tf_op jit(solution)/shard_map/ppermute | solution.py:16
  19.4 2.2 collective-permute-done.1
  22.8 4.2 %fusion.108 = (f32[12,288]{1,0:T(8,128)S(1)}, f32[12,288,288]{1,2,0:T(8,128)}) fusion(pred[288,288]{0,1:T(8,128)(4,1)S(1)} %broadcast_compare_fusion, bf16[1,288,3,12,32]{1,4,3,2,0:T(8,128)(2,1)S(1)} %bitcast.100), kind=kOutput, calls=%fused_computation.164 | convolution fusion | flops 67682592 | bytes 4695552 | tf_op jit(solution)/shard_map/sub | solution.py:109
  27.0 3.1 %fusion.36 = bf16[12,32,288]{2,1,0:T(8,128)(2,1)S(1)} fusion(bf16[1,288,3,12,32]{1,4,3,2,0:T(8,128)(2,1)S(1)} %bitcast.101, f32[12,288,288]{1,2,0:T(8,128)} %get-tuple-element.35, f32[12,288]{1,0:T(8,128)S(1)} %get-tuple-element.34), kind=kOutput, calls=%fused_computation.43 | convolution fusion | flops 65802240 | bytes 4521984 | tf_op jit(solution)/shard_map/bhqk,bkhe->bqhe/dot_general | solution.py:112
  32.9 7.8 %collective-permute-done.2 = bf16[3,6,8,384]{3,2,1,0:T(8,128)(2,1)S(1)} collective-permute-done((bf16[3,6,8,384]{3,2,1,0:T(8,128)(2,1)S(1)}, bf16[3,6,8,384]{3,2,1,0:T(8,128)(2,1)S(1)}, u32[]{:S(2)}, u32[]{:S(2)}) %collective-permute-start.2) | collective-permute-done | bytes 110624 | tf_op jit(solution)/shard_map/ppermute | solution.py:16
  41.6 3.6 %collective-permute-done.3 = bf16[6,3,8,384]{3,2,1,0:T(8,128)(2,1)S(1)} collective-permute-done((bf16[6,3,8,384]{3,2,1,0:T(8,128)(2,1)S(1)}, bf16[6,3,8,384]{3,2,1,0:T(8,128)(2,1)S(1)}, u32[]{:S(2)}, u32[]{:S(2)}) %collective-permute-start.3) | collective-permute-done | bytes 110624 | tf_op jit(solution)/shard_map/ppermute | solution.py:16
  46.7 2.0 convert_reduce_fusion
  51.6 2.1 collective-permute-start.4
  53.8 4.1 %fusion.39 = f32[1536,384]{1,0:T(8,128)} fusion(bf16[288,384]{1,0:T(8,128)(2,1)S(1)} %bitcast.110, f32[288,1536]{1,0:T(8,128)} %copy-done.7), kind=kOutput, calls=%fused_computation.45 | convolution fusion | flops 343719936 | bytes 4349952 | tf_op jit(solution)/shard_map/dot_general | solution.py:167
  58.1 2.2 fusion.111
  61.8 4.2 %fusion.33 = bf16[1,288,1,12,32]{1,4,3,2,0:T(8,128)(2,1)} fusion(bf16[288,12,32]{0,2,1:T(8,128)(2,1)} %bitcast.105, f32[12,288,288]{1,2,0:T(8,128)} %get-tuple-element.35, f32[12,288]{1,0:T(8,128)} %copy-done.27), kind=kOutput, calls=%fused_computation.42 | convolution fusion | flops 65691648 | bytes 4437504 | tf_op jit(solution)/shard_map/bhqk,bqhe->bkhe/dot_general | solution.py:134
  66.0 3.2 %fusion.80 = f32[12,288,288]{1,2,0:T(8,128)} fusion(bf16[288,12,32]{0,2,1:T(8,128)(2,1)S(1)} %bitcast.106, bf16[1,288,3,12,32]{1,4,3,2,0:T(8,128)(2,1)S(1)} %bitcast.102), kind=kOutput, calls=%fused_computation.104 | convolution fusion | flops 63700992 | bytes 4571136 | tf_op jit(solution)/shard_map/bqhe,bkhe->bhqk/dot_general | solution.py:131
  69.3 9.4 %fusion.30 = bf16[1,288,1,12,32]{1,4,3,2,0:T(8,128)(2,1)} fusion(f32[12,288,288]{1,2,0:T(8,128)} %fusion.80, bf16[1,288,3,12,32]{1,4,3,2,0:T(8,128)(2,1)S(1)} %bitcast.103, f32[12,288,288]{1,2,0:T(8,128)} %get-tuple-element.35, f32[12,288]{1,0:T(8,128)} %copy-done.27), kind=kOutput, calls=%fused_computation.41 | convolution fusion | flops 70672032 | bytes 21798912 | tf_op jit(solution)/shard_map/bhqk,bqhe->bkhe/dot_general | solution.py:142
  78.7 9.4 %fusion.27 = bf16[1,288,1,12,32]{1,4,3,2,0:T(8,128)(2,1)} fusion(f32[12,288,288]{1,2,0:T(8,128)} %fusion.80, bf16[1,288,3,12,32]{1,4,3,2,0:T(8,128)(2,1)S(1)} %bitcast.104, f32[12,288,288]{1,2,0:T(8,128)} %get-tuple-element.35, f32[12,288]{1,0:T(8,128)} %copy-done.27), kind=kOutput, calls=%fused_computation.40 | convolution fusion | flops 70672032 | bytes 21798912 | tf_op jit(solution)/shard_map/bhqk,bkhe->bqhe/dot_general | solution.py:139
  89.4 1.9 fusion.109
  92.5 4.4 %copy.36 = bf16[1,288,3,12,32]{4,3,2,1,0:T(8,128)(2,1)} copy(bf16[1,288,3,12,32]{1,4,3,2,0:T(8,128)(2,1)S(1)} %maximum_convert_fusion) | data formatting | bytes 1327104 | tf_op jit(solution)/shard_map/convert_element_type | solution.py:145
  96.9 5.2 %convert_element_type.139 = bf16[6,6,8,1152]{3,2,1,0:T(8,128)(2,1)} reshape(bf16[1,288,3,12,32]{4,3,2,1,0:T(8,128)(2,1)} %copy.36) | data formatting | bytes 1327104 | tf_op jit(solution)/shard_map/convert_element_type | solution.py:145
  104.0 10.6 %collective-permute-done.6 = bf16[3,6,8,384]{3,2,1,0:T(8,128)(2,1)S(1)} collective-permute-done((bf16[3,6,8,384]{3,2,1,0:T(8,128)(2,1)S(1)}, bf16[3,6,8,384]{3,2,1,0:T(8,128)(2,1)S(1)}, u32[]{:S(2)}, u32[]{:S(2)}) %collective-permute-start.6) | collective-permute-done | bytes 110624 | tf_op jit(solution)/shard_map/ppermute | solution.py:16
  115.8 4.9 %collective-permute-done.7 = bf16[6,3,8,384]{3,2,1,0:T(8,128)(2,1)S(1)} collective-permute-done((bf16[6,3,8,384]{3,2,1,0:T(8,128)(2,1)S(1)}, bf16[6,3,8,384]{3,2,1,0:T(8,128)(2,1)S(1)}, u32[]{:S(2)}, u32[]{:S(2)}) %collective-permute-start.7) | collective-permute-done | bytes 110624 | tf_op jit(solution)/shard_map/ppermute | solution.py:16
  121.0 38.2 %all-reduce = (f32[384]{0:T(512)S(1)}, f32[384]{0:T(512)S(1)}, f32[1536]{0:T(1024)S(1)}) all-reduce(f32[384]{0:T(512)S(1)} %get-tuple-element.10, f32[384]{0:T(512)} %get-tuple-element.8, f32[1536]{0:T(1024)} %get-tuple-element.38), channel_id=1, replica_groups=mesh['gx'=8,'gy'=4] {'gx','gy'}, use_global_device_ids=true, to_apply=%region_12.13 | all-reduce | flops 2304 | bytes 18432 | tf_op jit(solution)/shard_map/psum | solution.py:213
  162.2 98.9 %all-reduce.4.cloned.1.call-done = (f32[384,1152]{1,0:T(8,128)}, f32[384,384]{1,0:T(8,128)}, f32[384,1536]{1,0:T(8,128)}, f32[1536,384]{1,0:T(8,128)}) async-done(((f32[384,1152]{1,0:T(8,128)}, f32[384,384]{1,0:T(8,128)}, f32[384,1536]{1,0:T(8,128)}, f32[1536,384]{1,0:T(8,128)}), (f32[384,1152]{1,0:T(8,128)}, f32[384,384]{1,0:T(8,128)}, f32[384,1536]{1,0:T(8,128)}, ...) | async-done | bytes 7077904 | tf_op jit(solution)/shard_map/psum | solution.py:213
  261.1 2.7 multiply_reduce_fusion.3
  263.8 1.8 multiply_reduce_fusion.4
  273.4 2.6 multiply_convert_fusion.3
  (136 shorter events, 34.3 us)
Async XLA Ops:
  7.2 38.7 %copy-start = (bf16[384,1536]{1,0:T(8,128)(2,1)S(1)}, bf16[384,1536]{1,0:T(8,128)(2,1)}, u32[]{:S(2)}) copy-start(bf16[384,1536]{1,0:T(8,128)(2,1)} %param.17) | copy-start | bytes 3538948
  7.2 14.6 %copy-start.5 = (bf16[384,1152]{1,0:T(8,128)(2,1)S(1)}, bf16[384,1152]{1,0:T(8,128)(2,1)}, u32[]{:S(2)}) copy-start(bf16[384,1152]{1,0:T(8,128)(2,1)} %param.14) | copy-start | bytes 2654212
  7.2 253.9 %all-reduce.4.cloned.1.call-start = ((), (), s32[]{:S(2)}) async-start(), calls=%async_computation | async-start | bytes 14155776 | tf_op jit(solution)/shard_map/psum | solution.py:213
  10.7 8.4 %collective-permute-start = (bf16[3,6,8,384]{3,2,1,0:T(8,128)(2,1)S(1)}, bf16[3,6,8,384]{3,2,1,0:T(8,128)(2,1)S(1)}, u32[]{:S(2)}, u32[]{:S(2)}) collective-permute-start(bf16[3,6,8,384]{3,2,1,0:T(8,128)(2,1)S(1)} %get-tuple-element.33), channel_id=1, source_target_pairs={{0,28},{4,0},{8,4},{12,8},{16,12},{20,16},{24,20},{28,24},{1,29},{... | collective-permute-start | bytes 331784 | tf_op jit(solution)/shard_map/ppermute | solution.py:16
  19.2 2.5 collective-permute-start.1
  22.8 4.2 %copy-start.8 = (bf16[288,1152]{0,1:T(8,128)(2,1)}, bf16[288,1152]{0,1:T(8,128)(2,1)S(1)}, u32[]{:S(2)}) copy-start(bf16[288,1152]{0,1:T(8,128)(2,1)S(1)} %copy.29) | copy-start | bytes 1990660
  32.0 13.3 %copy-start.4 = (bf16[6,6,8,384]{3,2,1,0:T(8,128)(2,1)S(1)}, bf16[6,6,8,384]{3,2,1,0:T(8,128)(2,1)}, u32[]{:S(2)}) copy-start(bf16[6,6,8,384]{3,2,1,0:T(8,128)(2,1)} %param.10) | copy-start | bytes 663556
  32.4 13.4 %copy-start.19 = (f32[384]{0:T(512)S(1)}, f32[384]{0:T(512)}, u32[]{:S(2)}) copy-start(f32[384]{0:T(512)} %param.16) | copy-start | bytes 4612
  32.5 13.5 %copy-start.21 = (f32[1536]{0:T(1024)S(1)}, f32[1536]{0:T(1024)}, u32[]{:S(2)}) copy-start(f32[1536]{0:T(1024)} %param.18) | copy-start | bytes 18436
  32.5 8.2 %collective-permute-start.2 = (bf16[3,6,8,384]{3,2,1,0:T(8,128)(2,1)S(1)}, bf16[3,6,8,384]{3,2,1,0:T(8,128)(2,1)S(1)}, u32[]{:S(2)}, u32[]{:S(2)}) collective-permute-start(bf16[3,6,8,384]{3,2,1,0:T(8,128)(2,1)S(1)} %fusion.85), channel_id=1, source_target_pairs={{0,4},{4,8},{8,12},{12,16},{16,20},{20,24},{24,28},{28,0},{1,5},{5... | collective-permute-start | bytes 331784 | tf_op jit(solution)/shard_map/ppermute | solution.py:16
  40.8 4.5 %collective-permute-start.3 = (bf16[6,3,8,384]{3,2,1,0:T(8,128)(2,1)S(1)}, bf16[6,3,8,384]{3,2,1,0:T(8,128)(2,1)S(1)}, u32[]{:S(2)}, u32[]{:S(2)}) collective-permute-start(bf16[6,3,8,384]{3,2,1,0:T(8,128)(2,1)S(1)} %slice.203), channel_id=1, source_target_pairs={{0,1},{1,2},{2,3},{3,0},{4,5},{5,6},{6,7},{7,4},{8,9},{9,10},{10,1... | collective-permute-start | bytes 331784 | tf_op jit(solution)/shard_map/ppermute | solution.py:16
  51.6 6.5 %copy-start.16 = (bf16[288,1536]{1,0:T(8,128)(2,1)S(1)}, bf16[288,1536]{1,0:T(8,128)(2,1)}, u32[]{:S(2)}) copy-start(bf16[288,1536]{1,0:T(8,128)(2,1)} %copy-done.15) | copy-start | bytes 2654212
  51.6 6.2 %collective-permute-start.4 = (bf16[3,6,8,384]{3,2,1,0:T(8,128)(2,1)S(1)}, bf16[3,6,8,384]{3,2,1,0:T(8,128)(2,1)S(1)}, u32[]{:S(2)}, u32[]{:S(2)}) collective-permute-start(bf16[3,6,8,384]{3,2,1,0:T(8,128)(2,1)S(1)} %get-tuple-element.29), channel_id=1, source_target_pairs={{0,28},{4,0},{8,4},{12,8},{16,12},{20,16},{24,20},{28,24},{1,29},{... | collective-permute-start | bytes 331784 | tf_op jit(solution)/shard_map/ppermute | solution.py:16
  57.8 2.6 collective-permute-start.5
  96.9 5.2 %copy-start.6 = (bf16[384,1152]{1,0:T(8,128)(2,1)S(1)}, bf16[384,1152]{1,0:T(8,128)(2,1)}, u32[]{:S(2)}) copy-start(bf16[384,1152]{1,0:T(8,128)(2,1)} %param.14) | copy-start | bytes 2654212
  103.7 16.9 %copy-start.20 = (f32[384]{0:T(512)S(1)}, f32[384]{0:T(512)}, u32[]{:S(2)}) copy-start(f32[384]{0:T(512)} %param.13) | copy-start | bytes 4612
  103.7 57.4 %copy-start.18 = (bf16[6,6,8,384]{3,2,1,0:T(8,128)(2,1)S(1)}, bf16[6,6,8,384]{3,2,1,0:T(8,128)(2,1)}, u32[]{:S(2)}) copy-start(bf16[6,6,8,384]{3,2,1,0:T(8,128)(2,1)} %param.11) | copy-start | bytes 663556
  103.9 10.6 %collective-permute-start.6 = (bf16[3,6,8,384]{3,2,1,0:T(8,128)(2,1)S(1)}, bf16[3,6,8,384]{3,2,1,0:T(8,128)(2,1)S(1)}, u32[]{:S(2)}, u32[]{:S(2)}) collective-permute-start(bf16[3,6,8,384]{3,2,1,0:T(8,128)(2,1)S(1)} %fusion.83), channel_id=1, source_target_pairs={{0,4},{4,8},{8,12},{12,16},{16,20},{20,24},{24,28},{28,0},{1,5},{5... | collective-permute-start | bytes 331784 | tf_op jit(solution)/shard_map/ppermute | solution.py:16
  114.6 6.0 %collective-permute-start.7 = (bf16[6,3,8,384]{3,2,1,0:T(8,128)(2,1)S(1)}, bf16[6,3,8,384]{3,2,1,0:T(8,128)(2,1)S(1)}, u32[]{:S(2)}, u32[]{:S(2)}) collective-permute-start(bf16[6,3,8,384]{3,2,1,0:T(8,128)(2,1)S(1)} %slice.202), channel_id=1, source_target_pairs={{0,1},{1,2},{2,3},{3,0},{4,5},{5,6},{6,7},{7,4},{8,9},{9,10},{10,1... | collective-permute-start | bytes 331784 | tf_op jit(solution)/shard_map/ppermute | solution.py:16
  261.1 4.5 %copy-start.2 = (f32[384,1536]{1,0:T(8,128)S(1)}, f32[384,1536]{1,0:T(8,128)}, u32[]{:S(2)}) copy-start(f32[384,1536]{1,0:T(8,128)} %get-tuple-element.18) | copy-start | bytes 7077892
  261.1 5.7 %copy-start.1 = (f32[1536,384]{1,0:T(8,128)S(1)}, f32[1536,384]{1,0:T(8,128)}, u32[]{:S(2)}) copy-start(f32[1536,384]{1,0:T(8,128)} %get-tuple-element.19) | copy-start | bytes 7077892
  265.6 7.2 %copy-start.25 = (f32[384]{0:T(512)S(1)}, f32[384]{0:T(512)}, u32[]{:S(2)}) copy-start(f32[384]{0:T(512)} %copy-done.24) | copy-start | bytes 4612
  268.1 9.7 %copy-start.23 = (f32[384]{0:T(512)S(1)}, f32[384]{0:T(512)}, u32[]{:S(2)}) copy-start(f32[384]{0:T(512)} %copy-done.22) | copy-start | bytes 4612
  272.8 5.6 %copy-start.3 = (f32[384,1536]{1,0:T(8,128)S(1)}, f32[384,1536]{1,0:T(8,128)}, u32[]{:S(2)}) copy-start(f32[384,1536]{1,0:T(8,128)} %get-tuple-element.18) | copy-start | bytes 7077892
  (13 other events, 31.3 us)
Sparse Core Ops, SparseCore 0:
  92.6 168.4 all-reduce.3
where the time goes:
time: 289 us; the launch traced here: 288 us
  waiting for transfers between devices  130 us (45%)
  matrix products  49 us (17%)
  blocking collectives  38.2 us (13%)
  other arithmetic  27 us (9%)
  between operations  19.3 us (7%)
  local copies, waits for them, and re-layouts  14.4 us (5%)
  starting transfers between devices  11 us (4%)
    psum x1, waiting for transfers between devices, body(): lax.psum((local_grads[0], local_grads[1], local_grads[2], local_grads[3],...  98.9 us
    psum x1, blocking collectives, body(): lax.psum((local_grads[0], local_grads[1], local_grads[2], local_grads[3],...  38.2 us
    ppermute x8, waiting for transfers between devices, shifted(): lax.ppermute(shard, axis, [(i, (i + by) % size) for i in range(size)])  30.6 us
    ppermute x8, starting transfers between devices, shifted(): lax.ppermute(shard, axis, [(i, (i + by) % size) for i in range(size)])  10.9 us
    convert_element_type x2, local copies, waits for them, and re-layouts, attend_backward(): grad_packed = jnp.stack((grad_query, grad_key, grad_val), axis=2).astype(...  9.59 us
    dot_general x1, matrix products, attend_backward(): jnp.einsum('bhqk,bqhe->bkhe', grad_low, queries, preferred_element_type=j...  9.44 us
    dot_general x1, matrix products, attend_backward(): jnp.einsum('bhqk,bkhe->bqhe', grad_low, key_part, preferred_element_type=...  9.35 us
    reduce_sum x7, other arithmetic, body(): square_sum = square_sum + jnp.sum(grad_term * grad_term)  8.87 us
  transfers between devices with their start and end apart: 9, of which 8 were waited for; matrix products, arithmetic and copies ran while one was open for 8% of the time, Pallas kernels for 0%

commit v1 on v0

--- a/solution.py
+++ b/solution.py
@@ -210,7 +210,7 @@
     param_total = 0
     for grad_term in local_grads:
         param_total = param_total + math.prod(grad_term.shape)
-    summed = lax.psum(
+    half = lax.psum(
         (
             local_grads[0],
             local_grads[1],
@@ -220,8 +220,9 @@
             local_grads[5],
             local_grads[6],
         ),
-        ("gx", "gy"),
-    )
+        "gy",
+    )
+    summed = lax.psum(half, "gx")
     square_sum = jnp.zeros((), jnp.float32)
     for grad_term in summed:
         square_sum = square_sum + jnp.sum(grad_term * grad_term)

time: 289 us -> 497 us (1.72)
  waiting for transfers between devices: 130 us -> 329 us
  blocking collectives: 38.2 us -> 47.3 us
    psum x0 -> x1, waiting for transfers between devices: none -> 167 us  [body(): summed = lax.psum(half, 'gx')]
    psum x0 -> x1, blocking collectives: none -> 36.4 us  [body(): summed = lax.psum(half, 'gx')]
    psum x1, waiting for transfers between devices: 98.9 us -> 134 us  [body(): lax.psum((local_grads[0], local_grads[1], local_grads[2], local_grads[3],...]
    psum x1, blocking collectives: 38.2 us -> 10.9 us  [body(): lax.psum((local_grads[0], local_grads[1], local_grads[2], local_grads[3],...]
  transfers between devices with their start and end apart: 9 -> 10, of which waited for: 8 -> 9; matrix products, arithmetic and copies ran while one was open for 8% -> 4% of each run, Pallas kernels for 0% -> 0%
where the time goes in v1:
time: 497 us; the launch traced here: 496 us
  waiting for transfers between devices  329 us (66%)
  matrix products  49.2 us (10%)
  blocking collectives  47.3 us (10%)
  other arithmetic  26.4 us (5%)
  between operations  19.2 us (4%)
  local copies, waits for them, and re-layouts  14.2 us (3%)
  starting transfers between devices  11.3 us (2%)
    psum x1, waiting for transfers between devices, body(): summed = lax.psum(half, 'gx')  167 us
    psum x1, waiting for transfers between devices, body(): lax.psum((local_grads[0], local_grads[1], local_grads[2], local_grads[3],...  134 us
    psum x1, blocking collectives, body(): summed = lax.psum(half, 'gx')  36.4 us
    ppermute x8, waiting for transfers between devices, shifted(): lax.ppermute(shard, axis, [(i, (i + by) % size) for i in range(size)])  28.3 us
    ppermute x8, starting transfers between devices, shifted(): lax.ppermute(shard, axis, [(i, (i + by) % size) for i in range(size)])  11.2 us
    psum x1, blocking collectives, body(): lax.psum((local_grads[0], local_grads[1], local_grads[2], local_grads[3],...  10.9 us
  transfers between devices with their start and end apart: 10, of which 9 were waited for; matrix products, arithmetic and copies ran while one was open for 4% of the time, Pallas kernels for 0%

profile of v1, /device:TPU:0, one launch (start us, length us, event | category | flops | bytes accessed | tf_op | source)
XLA Modules:
  0.0 496.4 jit_solution(4262973085192381928)
XLA Ops:
  10.7 6.1 %collective-permute-start = (bf16[3,6,8,384]{3,2,1,0:T(8,128)(2,1)S(1)}, bf16[3,6,8,384]{3,2,1,0:T(8,128)(2,1)S(1)}, u32[]{:S(2)}, u32[]{:S(2)}) collective-permute-start(bf16[3,6,8,384]{3,2,1,0:T(8,128)(2,1)S(1)} %get-tuple-element.40), channel_id=1, source_target_pairs={{0,28},{4,0},{8,4},{12,8},{16,12},{20,16},{24,20},{28,24},{1,29},{... | collective-permute-start | bytes 331784 | tf_op jit(solution)/shard_map/ppermute | solution.py:16
  19.4 2.2 collective-permute-done.1
  22.8 4.2 fusion.108
  27.0 3.1 fusion.36
  32.9 7.8 %collective-permute-done.2 = bf16[3,6,8,384]{3,2,1,0:T(8,128)(2,1)S(1)} collective-permute-done((bf16[3,6,8,384]{3,2,1,0:T(8,128)(2,1)S(1)}, bf16[3,6,8,384]{3,2,1,0:T(8,128)(2,1)S(1)}, u32[]{:S(2)}, u32[]{:S(2)}) %collective-permute-start.2) | collective-permute-done | bytes 110624 | tf_op jit(solution)/shard_map/ppermute | solution.py:16
  41.6 3.6 collective-permute-done.3
  46.7 2.0 convert_reduce_fusion
  51.2 2.1 collective-permute-start.4
  53.3 4.1 fusion.39
  57.6 2.2 fusion.111
  61.4 4.2 fusion.33
  65.6 3.2 fusion.80
  68.8 9.4 %fusion.30 = bf16[1,288,1,12,32]{1,4,3,2,0:T(8,128)(2,1)} fusion(f32[12,288,288]{1,2,0:T(8,128)} %fusion.80, bf16[1,288,3,12,32]{1,4,3,2,0:T(8,128)(2,1)S(1)} %bitcast.103, f32[12,288,288]{1,2,0:T(8,128)} %get-tuple-element.42, f32[12,288]{1,0:T(8,128)} %copy-done.27), kind=kOutput, calls=%fused_computation.41 | convolution fusion | flops 70672032 | bytes 21798912 | tf_op jit(solution)/shard_map/bhqk,bqhe->bkhe/dot_general | solution.py:142
  78.2 9.4 %fusion.27 = bf16[1,288,1,12,32]{1,4,3,2,0:T(8,128)(2,1)} fusion(f32[12,288,288]{1,2,0:T(8,128)} %fusion.80, bf16[1,288,3,12,32]{1,4,3,2,0:T(8,128)(2,1)S(1)} %bitcast.104, f32[12,288,288]{1,2,0:T(8,128)} %get-tuple-element.42, f32[12,288]{1,0:T(8,128)} %copy-done.27), kind=kOutput, calls=%fused_computation.40 | convolution fusion | flops 70672032 | bytes 21798912 | tf_op jit(solution)/shard_map/bhqk,bkhe->bqhe/dot_general | solution.py:139
  92.1 133.9 %all-reduce.9.cloned.1.call-done = (f32[384,1152]{1,0:T(8,128)}, f32[384,384]{1,0:T(8,128)}, f32[384,1536]{1,0:T(8,128)}, f32[1536,384]{1,0:T(8,128)}) async-done(((f32[384,1152]{1,0:T(8,128)}, f32[384,384]{1,0:T(8,128)}, f32[384,1536]{1,0:T(8,128)}, f32[1536,384]{1,0:T(8,128)}), (f32[384,1152]{1,0:T(8,128)}, f32[384,384]{1,0:T(8,128)}, f32[384,1536]{1,0:T(8,128)}, ...) | async-done | bytes 7077904 | tf_op jit(solution)/shard_map/psum | solution.py:213
  226.1 4.4 copy.36
  230.5 5.0 %convert_element_type.139 = bf16[6,6,8,1152]{3,2,1,0:T(8,128)(2,1)} reshape(bf16[1,288,3,12,32]{4,3,2,1,0:T(8,128)(2,1)} %copy.36) | data formatting | bytes 1327104 | tf_op jit(solution)/shard_map/convert_element_type | solution.py:145
  238.9 9.0 %collective-permute-done.6 = bf16[3,6,8,384]{3,2,1,0:T(8,128)(2,1)S(1)} collective-permute-done((bf16[3,6,8,384]{3,2,1,0:T(8,128)(2,1)S(1)}, bf16[3,6,8,384]{3,2,1,0:T(8,128)(2,1)S(1)}, u32[]{:S(2)}, u32[]{:S(2)}) %collective-permute-start.6) | collective-permute-done | bytes 110624 | tf_op jit(solution)/shard_map/ppermute | solution.py:16
  248.1 4.1 collective-permute-done.7
  252.6 10.9 %all-reduce.2 = (f32[384]{0:T(512)S(1)}, f32[384]{0:T(512)S(1)}, f32[1536]{0:T(1024)S(1)}) all-reduce(f32[384]{0:T(512)S(1)} %get-tuple-element.10, f32[384]{0:T(512)S(1)} %get-tuple-element.8, f32[1536]{0:T(1024)} %get-tuple-element.45), channel_id=1, replica_groups=mesh['gx'=8,'gy'=4] {'gy'}, use_global_device_ids=true, to_apply=%region_12.13 | all-reduce | flops 2304 | bytes 18432 | tf_op jit(solution)/shard_map/psum | solution.py:213
  263.5 36.4 %all-reduce = (f32[384]{0:T(512)S(1)}, f32[384]{0:T(512)S(1)}, f32[1536]{0:T(1024)S(1)}) all-reduce(f32[384]{0:T(512)S(1)} %get-tuple-element.20, f32[384]{0:T(512)S(1)} %get-tuple-element.21, f32[1536]{0:T(1024)S(1)} %get-tuple-element.22), channel_id=1, replica_groups=mesh['gx'=8,'gy'=4] {'gx'}, use_global_device_ids=true, to_apply=%region_13.14 | all-reduce | flops 2304 | bytes 18432 | tf_op jit(solution)/shard_map/psum | solution.py:225
  303.0 166.6 %all-reduce.7.cloned.1.call-done = (f32[384,1152]{1,0:T(8,128)}, f32[384,384]{1,0:T(8,128)}, f32[384,1536]{1,0:T(8,128)}, f32[1536,384]{1,0:T(8,128)}) async-done(((f32[384,1152]{1,0:T(8,128)}, f32[384,384]{1,0:T(8,128)}, f32[384,1536]{1,0:T(8,128)}, f32[1536,384]{1,0:T(8,128)}), (f32[384,1152]{1,0:T(8,128)}, f32[384,384]{1,0:T(8,128)}, f32[384,1536]{1,0:T(8,128)}, ...) | async-done | bytes 7077904 | tf_op jit(solution)/shard_map/psum | solution.py:225
  469.5 2.7 multiply_reduce_fusion.3
  481.6 2.6 multiply_convert_fusion.3
  (140 shorter events, 38.0 us)
Async XLA Ops:
  7.2 38.7 %copy-start = (bf16[384,1536]{1,0:T(8,128)(2,1)S(1)}, bf16[384,1536]{1,0:T(8,128)(2,1)}, u32[]{:S(2)}) copy-start(bf16[384,1536]{1,0:T(8,128)(2,1)} %param.17) | copy-start | bytes 3538948
  7.2 14.6 %copy-start.5 = (bf16[384,1152]{1,0:T(8,128)(2,1)S(1)}, bf16[384,1152]{1,0:T(8,128)(2,1)}, u32[]{:S(2)}) copy-start(bf16[384,1152]{1,0:T(8,128)(2,1)} %param.14) | copy-start | bytes 2654212
  7.2 218.8 %all-reduce.9.cloned.1.call-start = ((), (), s32[]{:S(2)}) async-start(), calls=%async_computation.1 | async-start | bytes 14155776 | tf_op jit(solution)/shard_map/psum | solution.py:213
  10.7 8.4 %collective-permute-start = (bf16[3,6,8,384]{3,2,1,0:T(8,128)(2,1)S(1)}, bf16[3,6,8,384]{3,2,1,0:T(8,128)(2,1)S(1)}, u32[]{:S(2)}, u32[]{:S(2)}) collective-permute-start(bf16[3,6,8,384]{3,2,1,0:T(8,128)(2,1)S(1)} %get-tuple-element.40), channel_id=1, source_target_pairs={{0,28},{4,0},{8,4},{12,8},{16,12},{20,16},{24,20},{28,24},{1,29},{... | collective-permute-start | bytes 331784 | tf_op jit(solution)/shard_map/ppermute | solution.py:16
  19.2 2.5 collective-permute-start.1
  32.0 13.3 %copy-start.4 = (bf16[6,6,8,384]{3,2,1,0:T(8,128)(2,1)S(1)}, bf16[6,6,8,384]{3,2,1,0:T(8,128)(2,1)}, u32[]{:S(2)}) copy-start(bf16[6,6,8,384]{3,2,1,0:T(8,128)(2,1)} %param.10) | copy-start | bytes 663556
  32.4 13.4 %copy-start.19 = (f32[384]{0:T(512)S(1)}, f32[384]{0:T(512)}, u32[]{:S(2)}) copy-start(f32[384]{0:T(512)} %param.16) | copy-start | bytes 4612
  32.5 13.5 %copy-start.21 = (f32[1536]{0:T(1024)S(1)}, f32[1536]{0:T(1024)}, u32[]{:S(2)}) copy-start(f32[1536]{0:T(1024)} %param.18) | copy-start | bytes 18436
  32.5 8.2 %collective-permute-start.2 = (bf16[3,6,8,384]{3,2,1,0:T(8,128)(2,1)S(1)}, bf16[3,6,8,384]{3,2,1,0:T(8,128)(2,1)S(1)}, u32[]{:S(2)}, u32[]{:S(2)}) collective-permute-start(bf16[3,6,8,384]{3,2,1,0:T(8,128)(2,1)S(1)} %fusion.85), channel_id=1, source_target_pairs={{0,4},{4,8},{8,12},{12,16},{16,20},{20,24},{24,28},{28,0},{1,5},{5... | collective-permute-start | bytes 331784 | tf_op jit(solution)/shard_map/ppermute | solution.py:16
  40.8 4.5 collective-permute-start.3
  51.1 6.5 %copy-start.16 = (bf16[288,1536]{1,0:T(8,128)(2,1)S(1)}, bf16[288,1536]{1,0:T(8,128)(2,1)}, u32[]{:S(2)}) copy-start(bf16[288,1536]{1,0:T(8,128)(2,1)} %copy-done.15) | copy-start | bytes 2654212
  51.2 6.2 %collective-permute-start.4 = (bf16[3,6,8,384]{3,2,1,0:T(8,128)(2,1)S(1)}, bf16[3,6,8,384]{3,2,1,0:T(8,128)(2,1)S(1)}, u32[]{:S(2)}, u32[]{:S(2)}) collective-permute-start(bf16[3,6,8,384]{3,2,1,0:T(8,128)(2,1)S(1)} %get-tuple-element.36), channel_id=1, source_target_pairs={{0,28},{4,0},{8,4},{12,8},{16,12},{20,16},{24,20},{28,24},{1,29},{... | collective-permute-start | bytes 331784 | tf_op jit(solution)/shard_map/ppermute | solution.py:16
  57.4 2.6 collective-permute-start.5
  92.1 377.4 %all-reduce.7.cloned.1.call-start = ((), (), s32[]{:S(2)}) async-start(), calls=%async_computation | async-start | bytes 14155776 | tf_op jit(solution)/shard_map/psum | solution.py:225
  230.5 5.0 %copy-start.6 = (bf16[384,1152]{1,0:T(8,128)(2,1)S(1)}, bf16[384,1152]{1,0:T(8,128)(2,1)}, u32[]{:S(2)}) copy-start(bf16[384,1152]{1,0:T(8,128)(2,1)} %param.14) | copy-start | bytes 2654212
  237.3 14.9 %copy-start.20 = (f32[384]{0:T(512)S(1)}, f32[384]{0:T(512)}, u32[]{:S(2)}) copy-start(f32[384]{0:T(512)} %param.13) | copy-start | bytes 4612
  237.3 64.5 %copy-start.18 = (bf16[6,6,8,384]{3,2,1,0:T(8,128)(2,1)S(1)}, bf16[6,6,8,384]{3,2,1,0:T(8,128)(2,1)}, u32[]{:S(2)}) copy-start(bf16[6,6,8,384]{3,2,1,0:T(8,128)(2,1)} %param.11) | copy-start | bytes 663556
  237.5 10.4 %collective-permute-start.6 = (bf16[3,6,8,384]{3,2,1,0:T(8,128)(2,1)S(1)}, bf16[3,6,8,384]{3,2,1,0:T(8,128)(2,1)S(1)}, u32[]{:S(2)}, u32[]{:S(2)}) collective-permute-start(bf16[3,6,8,384]{3,2,1,0:T(8,128)(2,1)S(1)} %fusion.83), channel_id=1, source_target_pairs={{0,4},{4,8},{8,12},{12,16},{16,20},{20,24},{24,28},{28,0},{1,5},{5... | collective-permute-start | bytes 331784 | tf_op jit(solution)/shard_map/ppermute | solution.py:16
  248.0 4.2 collective-permute-start.7
  469.5 4.5 copy-start.2
  469.5 5.7 %copy-start.1 = (f32[1536,384]{1,0:T(8,128)S(1)}, f32[1536,384]{1,0:T(8,128)}, u32[]{:S(2)}) copy-start(f32[1536,384]{1,0:T(8,128)} %get-tuple-element.19) | copy-start | bytes 7077892
  474.0 7.0 %copy-start.25 = (f32[384]{0:T(512)S(1)}, f32[384]{0:T(512)}, u32[]{:S(2)}) copy-start(f32[384]{0:T(512)} %copy-done.24) | copy-start | bytes 4612
  476.4 9.6 %copy-start.23 = (f32[384]{0:T(512)S(1)}, f32[384]{0:T(512)}, u32[]{:S(2)}) copy-start(f32[384]{0:T(512)} %copy-done.22) | copy-start | bytes 4612
  481.0 5.6 %copy-start.3 = (f32[384,1536]{1,0:T(8,128)S(1)}, f32[384,1536]{1,0:T(8,128)}, u32[]{:S(2)}) copy-start(f32[384,1536]{1,0:T(8,128)} %get-tuple-element.18) | copy-start | bytes 7077892
  (14 other events, 35.6 us)
Sparse Core Ops, SparseCore 0:
  92.2 133.8 all-reduce.8
  230.5 239.0 all-reduce.6
